TPU v7x, 128 devices: a whole 4x4x4 slice. The times are simulated.
128 devices in a mesh: px: 16 (over y, x), py: 8 (over z, core).
Axes of the slice: x: 4, y: 4, z: 4, core: 2. Of those that a mesh axis runs over, the one named last changes fastest.
Arguments:
- node_latents: bfloat16 [256, 160, 512], P('px', 'py'), may hold values from -6 to 6
- fine_edges: bfloat16 [256, 160, 6, 512], P('px', 'py'), may hold values from -6 to 6
- long_edges: bfloat16 [20480, 512], P(('px', 'py')), may hold values from -6 to 6
- neighbours: int32 [256, 160, 6], P('px', 'py'), may hold values from 0 to 7, as said below
- coarse_slots: int32 [2560], P(('px', 'py')), may hold values from 0 to 319, as said below
- long_senders: int32 [20480], P(('px', 'py')), may hold values from 0 to 2559
- long_receivers: int32 [20480], P(('px', 'py')), may hold values from 0 to 2559, as said below
- edge_inner: bfloat16 [2, 1536, 512], replicated, may hold values from -0.15625 to 0.15625
- edge_outer: bfloat16 [2, 512, 512], replicated, may hold values from -0.25 to 0.25
- edge_gain: float32 [2, 512], replicated, may hold values from 0.5 to 1.5
- node_inner: bfloat16 [2, 1024, 512], replicated, may hold values from -0.1875 to 0.1875
- node_outer: bfloat16 [2, 512, 512], replicated, may hold values from -0.25 to 0.25
- node_gain: float32 [2, 512], replicated, may hold values from 0.5 to 1.5
Outputs:
- new_nodes: bfloat16 [256, 160, 512], P('px', 'py')
- new_fine: bfloat16 [256, 160, 6, 512], P('px', 'py')
- new_long: bfloat16 [20480, 512], P(('px', 'py'))
Inputs may be any that keep to these rules, and one draw needn't show every extreme that they name: `neighbours`: the 6 codes of one node are different. `coarse_slots`: the 20 entries of one device's block are different. `long_receivers`: among the 160 long edges of one device, at most 3 have receivers c with the same c // 20, and on every device some such group has exactly 3.
All inputs are finite; a program needn't handle non-finite values.
Results may differ from a plain program's by a relative error of at most 0.0095.
Values may be sent and summed in bfloat16 or wider, within the bound.
No kernel may reach another device: no remote copies, remote signals or barrier semaphores. Data moves between devices by JAX's collectives and lax.ppermute only.
A program may use at most 128 MiB of HBM per device.

v0:
```python
import jax
import jax.numpy as jnp
from jax import lax
from jax.sharding import PartitionSpec as P

EPSILON = 1e-05


def with_halo(cells, sides, width):
    for axis, dim in sides:
        count = lax.axis_size(axis)
        head = lax.slice_in_dim(cells, 0, width, axis=dim)
        tail = lax.slice_in_dim(cells, cells.shape[dim] - width, cells.shape[dim], axis=dim)
        cells = jnp.concatenate(
            [
                lax.ppermute(tail, axis, [(i, (i + 1) % count) for i in range(count)]),
                cells,
                lax.ppermute(head, axis, [((i + 1) % count, i) for i in range(count)]),
            ],
            axis=dim,
        )
    return cells


def layer_norm(values, gains):
    center = values - jnp.mean(values, axis=-1, keepdims=True)
    spread = jnp.mean(center * center, axis=-1, keepdims=True)
    return center * lax.rsqrt(spread + EPSILON) * gains


def finish(before, inner_sum, outer, gains):
    hidden = jax.nn.silu(inner_sum).astype(jnp.bfloat16)
    output = jnp.dot(hidden, outer, preferred_element_type=jnp.float32)
    return (before.astype(jnp.float32) + layer_norm(output, gains)).astype(jnp.bfloat16)


def extended_index(neighbours, patch_columns):
    shifted_code = neighbours + (neighbours >= 4).astype(jnp.int32)
    rows_here = lax.broadcasted_iota(jnp.int32, neighbours.shape, 0)
    cols_here = lax.broadcasted_iota(jnp.int32, neighbours.shape, 1)
    row_step = shifted_code // 3 - 1
    column_step = shifted_code % 3 - 1
    return ((rows_here + 1 + row_step) * (patch_columns + 2) + cols_here + 1 + column_step).reshape(
        -1
    )


def owner_sums(receivers, messages, coarse_count, devices):
    long_count, features = messages.shape
    capacity = (2 * long_count + devices - 1) // devices
    owners = receivers // coarse_count
    matches = (owners[:, None] == lax.iota(jnp.int32, devices)[None, :]).astype(jnp.int32)
    before = jnp.cumsum(matches, axis=0) - matches
    ranking = jnp.sum(before * matches, axis=1)
    placed = owners * capacity + ranking
    bucket = jnp.zeros((devices * capacity, features), jnp.bfloat16).at[placed].set(messages)
    labels = (
        jnp.full((devices * capacity,), coarse_count, jnp.int32)
        .at[placed]
        .set(receivers % coarse_count)
    )
    arrived, arrived_tags = (
        lax.all_to_all(
            bucket.reshape(devices, capacity, features),
            ("px", "py"),
            split_axis=0,
            concat_axis=0,
            tiled=True,
        ),
        lax.all_to_all(
            labels.astype(jnp.bfloat16).reshape(devices, capacity),
            ("px", "py"),
            split_axis=0,
            concat_axis=0,
            tiled=True,
        ),
    )
    tag_values = arrived_tags.reshape(-1).astype(jnp.int32)
    chooser = (tag_values[:, None] == lax.iota(jnp.int32, coarse_count)[None, :]).astype(
        jnp.bfloat16
    )
    return lax.dot_general(
        chooser,
        arrived.reshape(-1, features),
        (((0,), (0,)), ((), ())),
        preferred_element_type=jnp.float32,
    )


def shards(
    node_latents,
    fine_edges,
    long_edges,
    neighbours,
    coarse_slots,
    long_senders,
    long_receivers,
    edge_inner,
    edge_outer,
    edge_gain,
    node_inner,
    node_outer,
    node_gain,
):
    patch_rows, patch_columns, features = node_latents.shape
    degree = fine_edges.shape[2]
    coarse_count = coarse_slots.shape[0]
    layers = edge_inner.shape[0]
    devices = lax.axis_size("px") * lax.axis_size("py")
    patch_cells = patch_rows * patch_columns
    sender_index = extended_index(neighbours, patch_columns)
    latents = node_latents.reshape(patch_cells, features)
    fine_rows = fine_edges.reshape(patch_cells * degree, features)
    long_rows = long_edges
    for layer_index in range(layers):
        edge_part = edge_inner[layer_index, :features]
        send_part = edge_inner[layer_index, features : 2 * features]
        receive_part = edge_inner[layer_index, 2 * features :]
        own_coarse = jnp.take(latents, coarse_slots, axis=0)
        coarse = lax.all_gather(own_coarse, ("px", "py"), axis=0, tiled=True)
        padded = with_halo(
            latents.reshape(patch_rows, patch_columns, features), (("px", 0), ("py", 1)), 1
        )
        sender_terms = jnp.dot(
            padded.reshape(-1, features), send_part, preferred_element_type=jnp.float32
        )
        receiver_terms = jnp.dot(latents, receive_part, preferred_element_type=jnp.float32)
        inner_sum = jnp.dot(fine_rows, edge_part, preferred_element_type=jnp.float32) + jnp.take(
            sender_terms, sender_index, axis=0
        )
        inner_sum = (
            inner_sum.reshape(patch_cells, degree, -1) + receiver_terms[:, None, :]
        ).reshape(patch_cells * degree, -1)
        fine_rows = finish(fine_rows, inner_sum, edge_outer[layer_index], edge_gain[layer_index])
        long_sum = jnp.dot(long_rows, edge_part, preferred_element_type=jnp.float32)
        long_sum = long_sum + jnp.dot(
            jnp.take(coarse, long_senders, axis=0), send_part, preferred_element_type=jnp.float32
        )
        long_sum = long_sum + jnp.dot(
            jnp.take(coarse, long_receivers, axis=0),
            receive_part,
            preferred_element_type=jnp.float32,
        )
        long_rows = finish(long_rows, long_sum, edge_outer[layer_index], edge_gain[layer_index])
        coarse_sum = owner_sums(long_receivers, long_rows, coarse_count, devices)
        incoming = jnp.sum(
            fine_rows.reshape(patch_cells, degree, features), axis=1, dtype=jnp.float32
        )
        incoming = incoming.at[coarse_slots].add(coarse_sum).astype(jnp.bfloat16)
        node_sum = jnp.dot(
            latents, node_inner[layer_index, :features], preferred_element_type=jnp.float32
        )
        node_sum = node_sum + jnp.dot(
            incoming, node_inner[layer_index, features:], preferred_element_type=jnp.float32
        )
        latents = finish(latents, node_sum, node_outer[layer_index], node_gain[layer_index])
    return (
        latents.reshape(patch_rows, patch_columns, features),
        fine_rows.reshape(fine_edges.shape),
        long_rows,
    )


def solution(mesh):
    in_specs = (
        P("px", "py", None),
        P("px", "py", None, None),
        P(("px", "py"), None),
        P("px", "py", None),
        P(("px", "py")),
        P(("px", "py")),
        P(("px", "py")),
        P(),
        P(),
        P(),
        P(),
        P(),
        P(),
    )
    out_specs = (P("px", "py", None), P("px", "py", None, None), P(("px", "py"), None))
    return jax.shard_map(shards, mesh=mesh, in_specs=in_specs, out_specs=out_specs, check_vma=False)
```

profile of v0, /device:TPU:1, one launch (start us, length us, event | category | flops | bytes accessed | tf_op | source)
XLA Modules:
  0.0 250.8 jit_solution(7708276694184682371)
XLA Ops:
  7.3 1.8 fusion.141
  9.1 5.8 %collective-permute-start.1 = (bf16[1,20,512]{2,0,1:T(2,128)(2,1)}, bf16[1,20,512]{2,0,1:T(2,128)(2,1)S(1)}, u32[]{:S(2)}, u32[]{:S(2)}) collective-permute-start(bf16[1,20,512]{2,0,1:T(2,128)(2,1)} %get-tuple-element.22), channel_id=1, source_target_pairs={{8,0},{16,8},{24,16},{32,24},{40,32},{48,40},{56,48},{64,56},{72,6... | collective-permute-start | bytes 61448 | tf_op jit(solution)/shard_map/ppermute | solution.py:18
  14.9 1.2 copy.28
  20.0 1.1 scatter_custom_fusion
  22.0 10.6 %all-to-all-start = ((bf16[128,1,3]{2,1,0:T(2,128)(2,1)}), bf16[128,1,3]{2,1,0:T(2,128)(2,1)S(1)}, u32[]{:S(2)}, u32[]{:S(2)}) async-start(bf16[128,1,3]{2,1,0:T(2,128)(2,1)} %all_to_all.17), calls=%async_computation | async-start | bytes 131072 | tf_op jit(solution)/shard_map/all_to_all | solution.py:70
  36.1 1.3 fusion.38
  37.4 2.3 fusion.33
  39.6 2.2 fusion.42
  41.9 2.7 %copy.29 = bf16[16,20,6,512]{3,2,1,0:T(8,128)(2,1)S(1)} copy(bf16[16,20,6,512]{3,0,2,1:T(8,128)(2,1)} %param.20) | data formatting | bytes 3932160 | tf_op args[1]
  44.6 2.1 reshape.173
  46.6 4.1 %add.211 = f32[320,6,512]{2,1,0:T(8,128)} broadcast(f32[320,512]{1,0:T(8,128)} %fusion.33), dimensions={0,2} | broadcast | bytes 4587520 | tf_op jit(solution)/shard_map/add | solution.py:132
  50.7 5.6 %add.212 = f32[1920,512]{1,0:T(8,128)} reshape(f32[320,6,512]{2,1,0:T(8,128)} %add.211) | data formatting | bytes 7864320 | tf_op jit(solution)/shard_map/add | solution.py:132
  56.4 1.2 collective-permute-start.3
  58.6 1.5 collective-permute-done.3
  61.3 1.4 fusion.36
  62.7 6.2 %gather_fusion = f32[1920,512]{1,0:T(8,128)} fusion(f32[396,512]{1,0:T(8,128)S(1)} %fusion.36, s32[2048]{0:T(1024)S(1)} %pad_clamp_fusion), kind=kCustom, calls=%fused_computation.clone | custom fusion | bytes 7872000 | tf_op jit(solution)/shard_map/jit(_take)/gather | solution.py:128
  68.9 8.3 %fusion.144 = (f32[1920]{0:T(1024)S(1)}, f32[1920,512]{1,0:T(8,128)}) fusion(bf16[2,512,512]{2,1,0:T(8,128)(2,1)} %param.27, f32[1920,512]{1,0:T(8,128)} %add.212, f32[1920,512]{1,0:T(8,128)} %gather_fusion, bf16[1920,512]{1,0:T(8,128)(2,1)S(1)} %copy-done.2, pred[1920]{0:T(1024)(128)(4,1)S(1)} %copy-done.27, bf16[2,1536,512]{2,1,0:T(8,128)(2,1)} %param.26), kind=kOutput, calls=%fused_computation.210 | convolution fusion | flops 2022111360 | bytes 14820736 | tf_op jit(solution)/shard_map/dot_general | solution.py:33
  77.2 2.8 %multiply_reduce_fusion.1 = f32[1920]{0:T(1024)S(1)} fusion(f32[1920,512]{1,0:T(8,128)} %get-tuple-element.31, f32[1920]{0:T(1024)S(1)} %broadcast_multiply_fusion.1), kind=kLoop, calls=%fused_computation.21 | loop fusion | flops 2947200 | bytes 3947520 | tf_op jit(solution)/shard_map/reduce_sum | solution.py:27
  80.0 7.5 %all-gather.5.cloned.1.call-done = bf16[128,20,512]{2,1,0:T(8,128)(2,1)} async-done(((bf16[1,20,512]{2,1,0:T(8,128)(2,1)}), bf16[128,20,512]{2,1,0:T(8,128)(2,1)}) %all-gather.5.cloned.1.call-update) | async-done | bytes 2621456 | tf_op jit(solution)/shard_map/all_gather | solution.py:120
  87.5 3.6 %reshape.308 = bf16[2560,512]{1,0:T(8,128)(2,1)S(1)} reshape(bf16[128,20,512]{2,1,0:T(8,128)(2,1)} %all-gather.5.cloned.1.call-done) | data formatting | bytes 5242880
  91.2 1.6 gather_fusion.2
  92.8 1.6 gather_fusion.3
  94.4 1.4 convolution_add_fusion.5
  95.8 1.9 fusion.147
  98.1 1.4 scatter_custom_fusion.1
  99.6 1.0 reshape.178
  100.6 5.3 %all-to-all-start.1 = ((bf16[128,3,512]{2,1,0:T(4,128)(2,1)}), bf16[128,3,512]{2,1,0:T(4,128)(2,1)S(1)}, u32[]{:S(2)}, u32[]{:S(2)}) async-start(bf16[128,3,512]{2,1,0:T(4,128)(2,1)} %reshape.178), calls=%async_computation.1 | async-start | bytes 1048576 | tf_op jit(solution)/shard_map/all_to_all | solution.py:63
  106.1 3.4 %add_convert_fusion.1 = bf16[1920,512]{1,0:T(8,128)(2,1)S(1)} fusion(bf16[1920,512]{1,0:T(8,128)(2,1)} %reshape.173, f32[1920,512]{1,0:T(8,128)} %get-tuple-element.31, f32[512]{0:T(512)S(1)} %bitcast.134, f32[1920]{0:T(1024)S(1)} %add_rsqrt_fusion.1, f32[1920]{0:T(1024)S(1)} %broadcast_multiply_fusion.1), kind=kLoop, calls=%fused_computation.20 | loop fusion | flops 5898240 | bytes 7881728 | tf_op jit(solution)/shard_map/convert_element_type | solution.py:34
  109.5 2.8 %reshape.186 = f32[320,6,512]{2,1,0:T(8,128)} reshape(bf16[1920,512]{1,0:T(8,128)(2,1)S(1)} %add_convert_fusion.1) | data formatting | bytes 5898240 | tf_op jit(solution)/shard_map/convert_element_type | solution.py:146
  112.4 5.0 %reduce_sum.141 = f32[320,512]{1,0:T(8,128)} reduce(f32[320,6,512]{2,1,0:T(8,128)} %reshape.186, f32[]{:T(128)} %constant.121.clone.1), dimensions={1}, to_apply=%region_2.4 | reduce | flops 819200 | bytes 4587524 | tf_op jit(solution)/shard_map/reduce_sum | solution.py:146
  117.3 2.1 all-to-all-done.1
  119.4 1.1 reshape.179
  120.5 1.3 fusion.89
  121.8 2.6 %scatter_fusion = f32[320,512]{1,0:T(8,128)} fusion(f32[320,512]{1,0:T(8,128)} %reduce_sum.141, s32[20]{0:T(128)S(1)} %copy-done.19, f32[20,512]{1,0:T(8,128)S(1)} %fusion.89), kind=kCustom, calls=%fused_computation.10 | custom fusion | flops 10240 | bytes 122960 | tf_op jit(solution)/shard_map/scatter-add | solution.py:149
  124.4 2.3 fusion.152
  128.5 2.0 fusion.20
  131.0 2.2 fusion.24
  133.3 4.5 %collective-permute-start.5 = (bf16[1,20,512]{2,1,0:T(8,128)(2,1)S(1)}, bf16[1,20,512]{2,1,0:T(8,128)(2,1)S(1)}, u32[]{:S(2)}, u32[]{:S(2)}) collective-permute-start(bf16[1,20,512]{2,1,0:T(8,128)(2,1)S(1)} %get-tuple-element.19), channel_id=1, source_target_pairs={{8,0},{16,8},{24,16},{32,24},{40,32},{48,40},{56,48},{64,56},{72,6... | collective-permute-start | bytes 61448 | tf_op jit(solution)/shard_map/ppermute | solution.py:18
  137.8 0.9 collective-permute-done.5
  138.8 2.4 collective-permute-start.7
  141.2 1.4 fusion.15
  142.5 3.0 %add.231 = f32[320,6,512]{2,1,0:T(8,128)} broadcast(f32[320,512]{1,0:T(8,128)S(1)} %fusion.15), dimensions={0,2} | broadcast | bytes 4587520 | tf_op jit(solution)/shard_map/add | solution.py:132
  145.5 5.5 %add.232 = f32[1920,512]{1,0:T(8,128)} reshape(f32[320,6,512]{2,1,0:T(8,128)} %add.231) | data formatting | bytes 7864320 | tf_op jit(solution)/shard_map/add | solution.py:132
  151.5 1.4 fusion.18
  152.9 6.4 %gather_fusion.4 = f32[1920,512]{1,0:T(8,128)} fusion(f32[396,512]{1,0:T(8,128)S(1)} %fusion.18, s32[2048]{0:T(1024)} %copy-done.10), kind=kCustom, calls=%fused_computation.3.clone | custom fusion | bytes 7872000 | tf_op jit(solution)/shard_map/jit(_take)/gather | solution.py:128
  159.3 8.1 %fusion.157 = (f32[1920]{0:T(1024)S(1)}, f32[1920,512]{1,0:T(8,128)}) fusion(bf16[2,512,512]{2,1,0:T(8,128)(2,1)} %param.27, f32[1920,512]{1,0:T(8,128)} %add.232, f32[1920,512]{1,0:T(8,128)} %gather_fusion.4, pred[1920]{0:T(1024)(128)(4,1)S(1)} %copy-done.28, bf16[1920,512]{1,0:T(8,128)(2,1)S(1)} %add_convert_fusion.1, bf16[2,1536,512]{2,1,0:T(8,128)(2,1)} %param.26), kind=kOutput, calls=%fused_computation.213 | convolution fusion | flops 2022111360 | bytes 14820736 | tf_op jit(solution)/shard_map/dot_general | solution.py:33
  167.4 2.8 %multiply_reduce_fusion = f32[1920]{0:T(1024)S(1)} fusion(f32[1920,512]{1,0:T(8,128)} %get-tuple-element.37, f32[1920]{0:T(1024)S(1)} %broadcast_multiply_fusion), kind=kLoop, calls=%fused_computation.18 | loop fusion | flops 2947200 | bytes 3947520 | tf_op jit(solution)/shard_map/reduce_sum | solution.py:27
  170.3 24.0 %all-gather.7.cloned.1.call-done = bf16[128,20,512]{2,1,0:T(8,128)(2,1)} async-done(((bf16[1,20,512]{2,1,0:T(8,128)(2,1)}), bf16[128,20,512]{2,1,0:T(8,128)(2,1)}) %all-gather.7.cloned.1.call-update) | async-done | bytes 2621456 | tf_op jit(solution)/shard_map/all_gather | solution.py:120
  194.3 5.2 %reshape.310 = bf16[2560,512]{1,0:T(8,128)(2,1)} reshape(bf16[128,20,512]{2,1,0:T(8,128)(2,1)} %all-gather.7.cloned.1.call-done) | data formatting | bytes 5242880
  199.5 3.2 %gather_fusion.6 = bf16[160,512]{1,0:T(8,128)(2,1)S(1)} fusion(bf16[2560,512]{1,0:T(8,128)(2,1)} %reshape.310, s32[1024]{0:T(1024)} %copy-done.16), kind=kCustom, calls=%fused_computation.6.clone | custom fusion | bytes 328320 | tf_op jit(solution)/shard_map/jit(_take)/gather | solution.py:137
  202.7 3.2 %gather_fusion.7 = bf16[160,512]{1,0:T(8,128)(2,1)S(1)} fusion(bf16[2560,512]{1,0:T(8,128)(2,1)} %reshape.310, s32[1024]{0:T(1024)} %copy-done.15), kind=kCustom, calls=%fused_computation.7.clone | custom fusion | bytes 328320 | tf_op jit(solution)/shard_map/jit(_take)/gather | solution.py:140
  205.9 1.3 convolution_add_fusion.3
  207.3 1.8 fusion.160
  209.5 1.4 scatter_custom_fusion.3
  211.0 1.1 reshape.182
  212.0 5.7 %all-to-all-start.2 = ((bf16[128,3,512]{2,1,0:T(4,128)(2,1)}), bf16[128,3,512]{2,1,0:T(4,128)(2,1)}, u32[]{:S(2)}, u32[]{:S(2)}) async-start(bf16[128,3,512]{2,1,0:T(4,128)(2,1)} %reshape.182), calls=%async_computation.2 | async-start | bytes 1048576 | tf_op jit(solution)/shard_map/all_to_all | solution.py:63
  217.8 3.7 %add_convert_fusion = bf16[1920,512]{1,0:T(8,128)(2,1)} fusion(f32[1920,512]{1,0:T(8,128)} %get-tuple-element.37, f32[512]{0:T(512)S(1)} %bitcast.132, f32[1920]{0:T(1024)S(1)} %add_rsqrt_fusion, f32[1920]{0:T(1024)S(1)} %broadcast_multiply_fusion, bf16[1920,512]{1,0:T(8,128)(2,1)S(1)} %add_convert_fusion.1), kind=kLoop, calls=%fused_computation.17 | loop fusion | flops 5898240 | bytes 7881728 | tf_op jit(solution)/shard_map/convert_element_type | solution.py:34
  221.5 4.6 %reshape.189 = f32[320,6,512]{2,1,0:T(8,128)} reshape(bf16[1920,512]{1,0:T(8,128)(2,1)} %add_convert_fusion) | data formatting | bytes 5898240 | tf_op jit(solution)/shard_map/convert_element_type | solution.py:146
  226.1 2.3 reshape.185
  228.4 5.2 %reduce_sum.149 = f32[320,512]{1,0:T(8,128)} reduce(f32[320,6,512]{2,1,0:T(8,128)} %reshape.189, f32[]{:T(128)} %constant.121.clone.1), dimensions={1}, to_apply=%region_15.19 | reduce | flops 819200 | bytes 4587524 | tf_op jit(solution)/shard_map/reduce_sum | solution.py:146
  233.6 2.4 copy.36
  235.9 1.4 reshape.183
  237.6 2.7 %scatter_fusion.1 = f32[320,512]{1,0:T(8,128)} fusion(f32[320,512]{1,0:T(8,128)} %reduce_sum.149, s32[20]{0:T(128)S(1)} %copy-done.20, f32[20,512]{1,0:T(8,128)S(1)} %fusion.88), kind=kCustom, calls=%fused_computation.12 | custom fusion | flops 10240 | bytes 122960 | tf_op jit(solution)/shard_map/scatter-add | solution.py:149
  240.3 2.4 fusion.165
  (156 shorter events, 15.9 us)
Async XLA Ops:
  7.2 26.0 %copy-start.31 = (s32[160]{0:T(256)S(1)}, s32[160]{0:T(256)}, u32[]{:S(2)}) copy-start(s32[160]{0:T(256)} %param.25) | copy-start | bytes 1924
  7.2 25.5 %copy-start.11 = (s32[16,20,6]{1,0,2:T(8,128)S(1)}, s32[16,20,6]{1,0,2:T(8,128)}, u32[]{:S(2)}) copy-start(s32[16,20,6]{1,0,2:T(8,128)} %param.22) | copy-start | bytes 23044
  7.2 26.6 %copy-start.30 = (s32[160]{0:T(256)S(1)}, s32[160]{0:T(256)}, u32[]{:S(2)}) copy-start(s32[160]{0:T(256)} %param.24) | copy-start | bytes 1924
  7.2 27.1 %copy-start.21 = (f32[2,512]{1,0:T(2,128)S(1)}, f32[2,512]{1,0:T(2,128)}, u32[]{:S(2)}) copy-start(f32[2,512]{1,0:T(2,128)} %param.28) | copy-start | bytes 12292
  7.2 27.7 %copy-start.22 = (f32[2,512]{1,0:T(2,128)S(1)}, f32[2,512]{1,0:T(2,128)}, u32[]{:S(2)}) copy-start(f32[2,512]{1,0:T(2,128)} %param.31) | copy-start | bytes 12292
  7.2 28.9 %copy-start.7 = (bf16[160,512]{1,0:T(8,128)(2,1)S(1)}, bf16[160,512]{1,0:T(8,128)(2,1)}, u32[]{:S(2)}) copy-start(bf16[160,512]{1,0:T(8,128)(2,1)} %param.21) | copy-start | bytes 491524
  7.2 80.3 %all-gather.5.cloned.1.call-start = ((), (), s32[]{:S(2)}) async-start(), calls=%async_computation.3 | async-start | bytes 3170304 | tf_op jit(solution)/shard_map/all_gather | solution.py:120
  9.1 47.2 %collective-permute-start.1 = (bf16[1,20,512]{2,0,1:T(2,128)(2,1)}, bf16[1,20,512]{2,0,1:T(2,128)(2,1)S(1)}, u32[]{:S(2)}, u32[]{:S(2)}) collective-permute-start(bf16[1,20,512]{2,0,1:T(2,128)(2,1)} %get-tuple-element.22), channel_id=1, source_target_pairs={{8,0},{16,8},{24,16},{32,24},{40,32},{48,40},{56,48},{64,56},{72,6... | collective-permute-start | bytes 61448 | tf_op jit(solution)/shard_map/ppermute | solution.py:18
  14.9 41.5 %collective-permute-start = (bf16[1,20,512]{2,0,1:T(2,128)(2,1)S(1)}, bf16[1,20,512]{2,0,1:T(2,128)(2,1)S(1)}, u32[]{:S(2)}, u32[]{:S(2)}) collective-permute-start(bf16[1,20,512]{2,0,1:T(2,128)(2,1)S(1)} %get-tuple-element.21), channel_id=1, source_target_pairs={{0,8},{8,16},{16,24},{24,32},{32,40},{40,48},{48,56},{56,64},{64,7... | collective-permute-start | bytes 61448 | tf_op jit(solution)/shard_map/ppermute | solution.py:16
  16.7 3.0 %copy-start.18 = (s32[20]{0:T(128)}, s32[20]{0:T(128)S(1)}, u32[]{:S(2)}) copy-start(s32[20]{0:T(128)S(1)} %compare_select_fusion.4) | copy-start | bytes 244
  17.4 16.9 %copy-start.25 = (pred[20]{0:T(512)(128)(4,1)}, pred[20]{0:T(512)(128)(4,1)S(1)}, u32[]{:S(2)}) copy-start(pred[20]{0:T(512)(128)(4,1)S(1)} %compare_and_fusion.3) | copy-start | bytes 64
  20.0 13.1 %copy-start.29 = (s32[160]{0:T(256)}, s32[160]{0:T(256)S(1)}, u32[]{:S(2)}) copy-start(s32[160]{0:T(256)S(1)} %compare_select_fusion.3) | copy-start | bytes 1924
  22.0 36.2 %all-to-all-start = ((bf16[128,1,3]{2,1,0:T(2,128)(2,1)}), bf16[128,1,3]{2,1,0:T(2,128)(2,1)S(1)}, u32[]{:S(2)}, u32[]{:S(2)}) async-start(bf16[128,1,3]{2,1,0:T(2,128)(2,1)} %all_to_all.17), calls=%async_computation | async-start | bytes 131072 | tf_op jit(solution)/shard_map/all_to_all | solution.py:70
  33.2 29.5 %copy-start.10 = (s32[2048]{0:T(1024)}, s32[2048]{0:T(1024)S(1)}, u32[]{:S(2)}) copy-start(s32[2048]{0:T(1024)S(1)} %pad_clamp_fusion) | copy-start | bytes 24580
  41.9 49.3 %copy-start.16 = (s32[1024]{0:T(1024)}, s32[1024]{0:T(1024)S(1)}, u32[]{:S(2)}) copy-start(s32[1024]{0:T(1024)S(1)} %get-tuple-element.43) | copy-start | bytes 12292
  41.9 50.9 %copy-start.15 = (s32[1024]{0:T(1024)}, s32[1024]{0:T(1024)S(1)}, u32[]{:S(2)}) copy-start(s32[1024]{0:T(1024)S(1)} %get-tuple-element.42) | copy-start | bytes 12292
  50.7 5.6 %copy-start.3 = (bf16[16,20,512]{2,0,1:T(8,128)(2,1)S(1)}, bf16[16,20,512]{2,0,1:T(8,128)(2,1)}, u32[]{:S(2)}) copy-start(bf16[16,20,512]{2,0,1:T(8,128)(2,1)} %param.19) | copy-start | bytes 983044
  56.4 3.7 %collective-permute-start.3 = (bf16[18,1,512]{2,0,1:T(8,128)(2,1)S(1)}, bf16[18,1,512]{2,0,1:T(8,128)(2,1)S(1)}, u32[]{:S(2)}, u32[]{:S(2)}) collective-permute-start(bf16[18,1,512]{2,0,1:T(8,128)(2,1)S(1)} %get-tuple-element.18), channel_id=1, source_target_pairs={{1,0},{2,1},{3,2},{4,3},{5,4},{6,5},{7,6},{0,7},{9,8},{10,9},{11,1... | collective-permute-start | bytes 55304 | tf_op jit(solution)/shard_map/ppermute | solution.py:18
  57.6 3.1 %collective-permute-start.2 = (bf16[18,1,512]{2,0,1:T(8,128)(2,1)S(1)}, bf16[18,1,512]{2,0,1:T(8,128)(2,1)S(1)}, u32[]{:S(2)}, u32[]{:S(2)}) collective-permute-start(bf16[18,1,512]{2,0,1:T(8,128)(2,1)S(1)} %get-tuple-element.17), channel_id=1, source_target_pairs={{0,1},{1,2},{2,3},{3,4},{4,5},{5,6},{6,7},{7,0},{8,9},{9,10},{10,1... | collective-permute-start | bytes 55304 | tf_op jit(solution)/shard_map/ppermute | solution.py:16
  58.6 61.9 %copy-start.12 = (s32[384]{0:T(512)}, s32[384]{0:T(512)S(1)}, u32[]{:S(2)}) copy-start(s32[384]{0:T(512)S(1)} %reshape.188) | copy-start | bytes 4612
  62.7 6.2 %copy-start.2 = (bf16[1920,512]{1,0:T(8,128)(2,1)S(1)}, bf16[1920,512]{1,0:T(8,128)(2,1)}, u32[]{:S(2)}) copy-start(bf16[1920,512]{1,0:T(8,128)(2,1)} %reshape.173) | copy-start | bytes 5898244
  62.7 6.2 %copy-start.27 = (pred[1920]{0:T(1024)(128)(4,1)S(1)}, pred[1920]{0:T(1024)(128)(4,1)}, u32[]{:S(2)}) copy-start(pred[1920]{0:T(1024)(128)(4,1)} %compare_and_fusion) | copy-start | bytes 5764
  80.0 14.4 %copy-start.23 = (pred[160]{0:T(512)(128)(4,1)S(1)}, pred[160]{0:T(512)(128)(4,1)}, u32[]{:S(2)}) copy-start(pred[160]{0:T(512)(128)(4,1)} %compare_and_fusion.2) | copy-start | bytes 484
  91.2 4.7 %copy-start.32 = (pred[160]{0:T(512)(128)(4,1)S(1)}, pred[160]{0:T(512)(128)(4,1)}, u32[]{:S(2)}) copy-start(pred[160]{0:T(512)(128)(4,1)} %compare_and_fusion.1) | copy-start | bytes 484
  92.8 5.2 %copy-start.8 = (bf16[160,512]{1,0:T(8,128)(2,1)S(1)}, bf16[160,512]{1,0:T(8,128)(2,1)}, u32[]{:S(2)}) copy-start(bf16[160,512]{1,0:T(8,128)(2,1)} %param.21) | copy-start | bytes 491524
  98.1 30.4 %copy-start.4 = (bf16[160,512]{1,0:T(8,128)(2,1)}, bf16[160,512]{1,0:T(8,128)(2,1)S(1)}, u32[]{:S(2)}) copy-start(bf16[160,512]{1,0:T(8,128)(2,1)S(1)} %add_convert_fusion.5) | copy-start | bytes 491524
  100.6 18.8 %all-to-all-start.1 = ((bf16[128,3,512]{2,1,0:T(4,128)(2,1)}), bf16[128,3,512]{2,1,0:T(4,128)(2,1)S(1)}, u32[]{:S(2)}, u32[]{:S(2)}) async-start(bf16[128,3,512]{2,1,0:T(4,128)(2,1)} %reshape.178), calls=%async_computation.1 | async-start | bytes 1048576 | tf_op jit(solution)/shard_map/all_to_all | solution.py:63
  105.9 88.4 %all-gather.7.cloned.1.call-start = ((), (), s32[]{:S(2)}) async-start(), calls=%async_computation.4 | async-start | bytes 3170304 | tf_op jit(solution)/shard_map/all_gather | solution.py:120
  112.4 9.4 %copy-start.19 = (s32[20]{0:T(128)S(1)}, s32[20]{0:T(128)}, u32[]{:S(2)}) copy-start(s32[20]{0:T(128)} %copy-done.18) | copy-start | bytes 244
  124.4 3.4 %copy-start.26 = (pred[20]{0:T(512)(128)(4,1)S(1)}, pred[20]{0:T(512)(128)(4,1)}, u32[]{:S(2)}) copy-start(pred[20]{0:T(512)(128)(4,1)} %copy-done.25) | copy-start | bytes 64
  130.6 7.2 %collective-permute-start.4 = (bf16[1,20,512]{2,1,0:T(8,128)(2,1)S(1)}, bf16[1,20,512]{2,1,0:T(8,128)(2,1)S(1)}, u32[]{:S(2)}, u32[]{:S(2)}) collective-permute-start(bf16[1,20,512]{2,1,0:T(8,128)(2,1)S(1)} %get-tuple-element.20), channel_id=1, source_target_pairs={{0,8},{8,16},{16,24},{24,32},{32,40},{40,48},{48,56},{56,64},{64,7... | collective-permute-start | bytes 61448 | tf_op jit(solution)/shard_map/ppermute | solution.py:16
  133.3 5.4 %collective-permute-start.5 = (bf16[1,20,512]{2,1,0:T(8,128)(2,1)S(1)}, bf16[1,20,512]{2,1,0:T(8,128)(2,1)S(1)}, u32[]{:S(2)}, u32[]{:S(2)}) collective-permute-start(bf16[1,20,512]{2,1,0:T(8,128)(2,1)S(1)} %get-tuple-element.19), channel_id=1, source_target_pairs={{8,0},{16,8},{24,16},{32,24},{40,32},{48,40},{56,48},{64,56},{72,6... | collective-permute-start | bytes 61448 | tf_op jit(solution)/shard_map/ppermute | solution.py:18
  138.8 12.3 %collective-permute-start.7 = (bf16[18,1,512]{2,1,0:T(2,128)(2,1)S(1)}, bf16[18,1,512]{2,1,0:T(2,128)(2,1)S(1)}, u32[]{:S(2)}, u32[]{:S(2)}) collective-permute-start(bf16[18,1,512]{2,1,0:T(2,128)(2,1)S(1)} %get-tuple-element.16), channel_id=1, source_target_pairs={{1,0},{2,1},{3,2},{4,3},{5,4},{6,5},{7,6},{0,7},{9,8},{10,9},{11,1... | collective-permute-start | bytes 55304 | tf_op jit(solution)/shard_map/ppermute | solution.py:18
  141.2 9.9 %collective-permute-start.6 = (bf16[18,1,512]{2,1,0:T(2,128)(2,1)S(1)}, bf16[18,1,512]{2,1,0:T(2,128)(2,1)S(1)}, u32[]{:S(2)}, u32[]{:S(2)}) collective-permute-start(bf16[18,1,512]{2,1,0:T(2,128)(2,1)S(1)} %get-tuple-element.15), channel_id=1, source_target_pairs={{0,1},{1,2},{2,3},{3,4},{4,5},{5,6},{6,7},{7,0},{8,9},{9,10},{10,1... | collective-permute-start | bytes 55304 | tf_op jit(solution)/shard_map/ppermute | solution.py:16
  152.9 6.4 %copy-start.28 = (pred[1920]{0:T(1024)(128)(4,1)S(1)}, pred[1920]{0:T(1024)(128)(4,1)}, u32[]{:S(2)}) copy-start(pred[1920]{0:T(1024)(128)(4,1)} %compare_and_fusion) | copy-start | bytes 5764
  170.2 35.7 %copy-start.6 = (f32[160,512]{1,0:T(8,128)S(1)}, f32[160,512]{1,0:T(8,128)}, u32[]{:S(2)}) copy-start(f32[160,512]{1,0:T(8,128)} %fusion.20) | copy-start | bytes 983044
  170.2 35.7 %copy-start.24 = (pred[160]{0:T(512)(128)(4,1)S(1)}, pred[160]{0:T(512)(128)(4,1)}, u32[]{:S(2)}) copy-start(pred[160]{0:T(512)(128)(4,1)} %compare_and_fusion.2) | copy-start | bytes 484
  199.5 7.8 %copy-start.33 = (pred[160]{0:T(512)(128)(4,1)S(1)}, pred[160]{0:T(512)(128)(4,1)}, u32[]{:S(2)}) copy-start(pred[160]{0:T(512)(128)(4,1)} %compare_and_fusion.1) | copy-start | bytes 484
  202.7 6.7 %copy-start.5 = (bf16[160,512]{1,0:T(8,128)(2,1)S(1)}, bf16[160,512]{1,0:T(8,128)(2,1)}, u32[]{:S(2)}) copy-start(bf16[160,512]{1,0:T(8,128)(2,1)} %copy-done.4) | copy-start | bytes 491524
  202.7 6.7 %copy-start.14 = (f32[1,512]{1,0:T(1,128)S(1)}, f32[1,512]{1,0:T(1,128)}, u32[]{:S(2)}) copy-start(f32[1,512]{1,0:T(1,128)} %get-tuple-element.25) | copy-start | bytes 6148
  209.5 12.0 %copy-start.9 = (bf16[160,512]{1,0:T(8,128)(2,1)}, bf16[160,512]{1,0:T(8,128)(2,1)S(1)}, u32[]{:S(2)}) copy-start(bf16[160,512]{1,0:T(8,128)(2,1)S(1)} %add_convert_fusion.4) | copy-start | bytes 491524
  212.0 23.9 %all-to-all-start.2 = ((bf16[128,3,512]{2,1,0:T(4,128)(2,1)}), bf16[128,3,512]{2,1,0:T(4,128)(2,1)}, u32[]{:S(2)}, u32[]{:S(2)}) async-start(bf16[128,3,512]{2,1,0:T(4,128)(2,1)} %reshape.182), calls=%async_computation.2 | async-start | bytes 1048576 | tf_op jit(solution)/shard_map/all_to_all | solution.py:63
  221.5 4.7 %copy-start = (bf16[1920,512]{1,0:T(8,128)(2,1)S(1)}, bf16[1920,512]{1,0:T(8,128)(2,1)}, u32[]{:S(2)}) copy-start(bf16[1920,512]{1,0:T(8,128)(2,1)} %add_convert_fusion) | copy-start | bytes 5898244
  228.4 5.2 %copy-start.1 = (bf16[16,20,6,512]{3,2,1,0:T(8,128)(2,1)S(1)}, bf16[16,20,6,512]{3,2,1,0:T(8,128)(2,1)}, u32[]{:S(2)}) copy-start(bf16[16,20,6,512]{3,2,1,0:T(8,128)(2,1)} %reshape.185) | copy-start | bytes 5898244
  233.6 3.8 %copy-start.13 = (s32[384]{0:T(512)S(1)}, s32[384]{0:T(512)}, u32[]{:S(2)}) copy-start(s32[384]{0:T(512)} %copy-done.12) | copy-start | bytes 4612
  233.6 4.1 %copy-start.20 = (s32[20]{0:T(128)S(1)}, s32[20]{0:T(128)}, u32[]{:S(2)}) copy-start(s32[20]{0:T(128)} %copy-done.18) | copy-start | bytes 244
  237.6 5.3 %copy-start.17 = (f32[1,512]{1,0:T(1,128)S(1)}, f32[1,512]{1,0:T(1,128)}, u32[]{:S(2)}) copy-start(f32[1,512]{1,0:T(1,128)} %get-tuple-element.23) | copy-start | bytes 6148
Sparse Core Ops, SparseCore 0:
  18.9 68.5 all-gather.4
  128.7 65.5 all-gather.6
where the time goes:
time: 253 us; the launch traced here: 251 us
  local copies, waits for them, and re-layouts  83.1 us (33%)
  matrix products  43.4 us (17%)
  starting transfers between devices  36.8 us (15%)
  waiting for transfers between devices  36.7 us (15%)
  other arithmetic  36.1 us (14%)
  between operations  14.7 us (6%)
    all_gather x2, waiting for transfers between devices, shards(): coarse = lax.all_gather(own_coarse, ('px', 'py'), axis=0, tiled=True)  31.5 us
    dot_general x6, matrix products, finish(): output = jnp.dot(hidden, outer, preferred_element_type=jnp.float32)  24.9 us
    add x4, local copies, waits for them, and re-layouts, shards(): inner_sum.reshape(patch_cells, degree, -1) + receiver_terms[:, None, :]  18.3 us
    unnamed x77, local copies, waits for them, and re-layouts  16 us
    ppermute x4, starting transfers between devices, with_halo(): lax.ppermute(head, axis, [((i + 1) % count, i) for i in range(count)])  13.8 us
    gather x2, local copies, waits for them, and re-layouts, shards(): jnp.take(sender_terms, sender_index, axis=0)  12.6 us
    all_to_all x2, starting transfers between devices, owner_sums(): lax.all_to_all(bucket.reshape(devices, capacity, features), ('px', 'py'),...  11 us
    all_to_all x1, starting transfers between devices, owner_sums(): lax.all_to_all(labels.astype(jnp.bfloat16).reshape(devices, capacity), ('...  10.6 us
  transfers between devices with their start and end apart: 13, of which 6 were waited for; matrix products, arithmetic and copies ran while one was open for 45% of the time, Pallas kernels for 0%

commit v1 on v0

--- a/solution.py
+++ b/solution.py
@@ -1,9 +1,26 @@
+import functools
 import jax
 import jax.numpy as jnp
 from jax import lax
 from jax.sharding import PartitionSpec as P
+from jax.lax import all_to_all, axis_size
 
 EPSILON = 1e-05
+
+
+def apply_trees(in_array, peer_axis):
+    return jnp.concatenate(
+        all_to_all(
+            jnp.stack(tuple((in_array for _ in range(axis_size(peer_axis)))), axis=0),
+            peer_axis,
+            0,
+            0,
+        ),
+        0,
+    )
+
+
+tell_the_routes_all = functools.partial(apply_trees, peer_axis=("px", "py"))
 
 
 def with_halo(cells, sides, width):
@@ -117,7 +134,7 @@
         send_part = edge_inner[layer_index, features : 2 * features]
         receive_part = edge_inner[layer_index, 2 * features :]
         own_coarse = jnp.take(latents, coarse_slots, axis=0)
-        coarse = lax.all_gather(own_coarse, ("px", "py"), axis=0, tiled=True)
+        coarse = tell_the_routes_all(own_coarse)
         padded = with_halo(
             latents.reshape(patch_rows, patch_columns, features), (("px", 0), ("py", 1)), 1
         )

time: 253 us -> 274 us (1.083)
  starting transfers between devices: 36.8 us -> 84.3 us
  waiting for transfers between devices: 36.7 us -> 18.9 us
  between operations: 14.7 us -> 1.38 us
  local copies, waits for them, and re-layouts: 83.1 us -> 86.6 us
    all_gather x2 -> x0, waiting for transfers between devices: 31.5 us -> none  [shards(): coarse = lax.all_gather(own_coarse, ('px', 'py'), axis=0, tiled=True)]
    all_to_all x2, starting transfers between devices: 11 us -> 42.2 us  [owner_sums(): lax.all_to_all(bucket.reshape(devices, capacity, features), ('px', 'py'),...]
    all_to_all x0 -> x2, starting transfers between devices: none -> 17.2 us  [apply_trees(): all_to_all(jnp.stack(tuple((in_array for _ in range(axis_size(peer_axis))...]
    all_to_all x0 -> x2, waiting for transfers between devices: none -> 10.1 us  [apply_trees(): all_to_all(jnp.stack(tuple((in_array for _ in range(axis_size(peer_axis))...]
    reshape x0 -> x2, local copies, waits for them, and re-layouts: none -> 8.81 us  [apply_trees(): jnp.concatenate(all_to_all(jnp.stack(tuple((in_array for _ in range(axis_...]
    unnamed x77 -> x69, local copies, waits for them, and re-layouts: 16 us -> 7.21 us
    ppermute x4, waiting for transfers between devices: 2.37 us -> 8.5 us  [with_halo(): lax.ppermute(head, axis, [((i + 1) % count, i) for i in range(count)])]
    another operation x3 -> x5, local copies, waits for them, and re-layouts: 0.02 us -> 3.75 us  [the longest x2 3.73 us: apply_trees(): jnp.stack(tuple((in_array for _ in range(axis_size(peer_axis)))), axis=0)]
  transfers between devices with their start and end apart: 13 -> 13, of which waited for: 6 -> 3; matrix products, arithmetic and copies ran while one was open for 45% -> 42% of each run, Pallas kernels for 0% -> 0%
where the time goes in v1:
time: 274 us; the launch traced here: 272 us
  local copies, waits for them, and re-layouts  86.6 us (32%)
  starting transfers between devices  84.3 us (31%)
  matrix products  43.1 us (16%)
  other arithmetic  37.6 us (14%)
  waiting for transfers between devices  18.9 us (7%)
    all_to_all x2, starting transfers between devices, owner_sums(): lax.all_to_all(bucket.reshape(devices, capacity, features), ('px', 'py'),...  42.2 us
    dot_general x6, matrix products, finish(): output = jnp.dot(hidden, outer, preferred_element_type=jnp.float32)  24.6 us
    add x4, local copies, waits for them, and re-layouts, shards(): inner_sum.reshape(patch_cells, degree, -1) + receiver_terms[:, None, :]  18.2 us
    all_to_all x2, starting transfers between devices, apply_trees(): all_to_all(jnp.stack(tuple((in_array for _ in range(axis_size(peer_axis))...  17.2 us
    gather x2, local copies, waits for them, and re-layouts, shards(): jnp.take(sender_terms, sender_index, axis=0)  12.6 us
    ppermute x4, starting transfers between devices, with_halo(): lax.ppermute(head, axis, [((i + 1) % count, i) for i in range(count)])  12.2 us
    all_to_all x1, starting transfers between devices, owner_sums(): lax.all_to_all(labels.astype(jnp.bfloat16).reshape(devices, capacity), ('...  10.6 us
    reduce_sum x2, other arithmetic, shards(): jnp.sum(fine_rows.reshape(patch_cells, degree, features), axis=1, dtype=j...  10.1 us
  transfers between devices with their start and end apart: 13, of which 3 were waited for; matrix products, arithmetic and copies ran while one was open for 42% of the time, Pallas kernels for 0%

profile of v1, /device:TPU:1, one launch (start us, length us, event | category | flops | bytes accessed | tf_op | source)
XLA Modules:
  0.0 271.9 jit_solution(11541631771451357886)
XLA Ops:
  0.6 1.7 fusion.141
  2.3 5.8 %collective-permute-start.1 = (bf16[1,20,512]{2,0,1:T(2,128)(2,1)}, bf16[1,20,512]{2,0,1:T(2,128)(2,1)S(1)}, u32[]{:S(2)}, u32[]{:S(2)}) collective-permute-start(bf16[1,20,512]{2,0,1:T(2,128)(2,1)} %get-tuple-element.22), channel_id=1, source_target_pairs={{8,0},{16,8},{24,16},{32,24},{40,32},{48,40},{56,48},{64,56},{72,6... | collective-permute-start | bytes 61448 | tf_op jit(solution)/shard_map/ppermute | solution.py:35
  11.3 10.6 %all-to-all-start = ((bf16[128,1,3]{2,1,0:T(2,128)(2,1)}), bf16[128,1,3]{2,1,0:T(2,128)(2,1)S(1)}, u32[]{:S(2)}, u32[]{:S(2)}) async-start(bf16[128,1,3]{2,1,0:T(2,128)(2,1)} %all_to_all.25), calls=%async_computation | async-start | bytes 131072 | tf_op jit(solution)/shard_map/all_to_all | solution.py:87
  22.0 1.2 copy.28
  27.0 1.2 compare_and_fusion.2
  28.2 1.3 compare_and_fusion.1
  29.5 2.2 fusion.42
  31.8 2.2 fusion.33
  34.6 1.3 fusion.38
  37.2 1.9 stack.4
  39.0 10.2 %all-to-all-start.1 = ((bf16[128,20,512]{2,1,0:T(8,128)(2,1)}), bf16[128,20,512]{2,1,0:T(8,128)(2,1)}, u32[]{:S(2)}, u32[]{:S(2)}) async-start(bf16[128,20,512]{2,1,0:T(8,128)(2,1)} %stack.4), calls=%async_computation.1 | async-start | bytes 6291456 | tf_op jit(solution)/shard_map/all_to_all | solution.py:13
  49.3 2.7 copy.29
  51.9 2.1 reshape.183
  54.0 4.1 %add.211 = f32[320,6,512]{2,1,0:T(8,128)} broadcast(f32[320,512]{1,0:T(8,128)} %fusion.33), dimensions={0,2} | broadcast | bytes 4587520 | tf_op jit(solution)/shard_map/add | solution.py:149
  58.1 5.6 %add.212 = f32[1920,512]{1,0:T(8,128)} reshape(f32[320,6,512]{2,1,0:T(8,128)} %add.211) | data formatting | bytes 7864320 | tf_op jit(solution)/shard_map/add | solution.py:149
  63.7 1.3 collective-permute-start.3
  66.0 8.5 %collective-permute-done.3 = bf16[18,1,512]{2,0,1:T(8,128)(2,1)S(1)} collective-permute-done((bf16[18,1,512]{2,0,1:T(8,128)(2,1)S(1)}, bf16[18,1,512]{2,0,1:T(8,128)(2,1)S(1)}, u32[]{:S(2)}, u32[]{:S(2)}) %collective-permute-start.3) | collective-permute-done | bytes 18464 | tf_op jit(solution)/shard_map/ppermute | solution.py:35
  75.0 1.4 fusion.36
  76.4 6.2 %gather_fusion = f32[1920,512]{1,0:T(8,128)} fusion(f32[396,512]{1,0:T(8,128)S(1)} %fusion.36, s32[2048]{0:T(1024)S(1)} %pad_clamp_fusion), kind=kCustom, calls=%fused_computation.clone | custom fusion | bytes 7872000 | tf_op jit(solution)/shard_map/jit(_take)/gather | solution.py:145
  82.6 8.1 %fusion.144 = (f32[1920]{0:T(1024)S(1)}, f32[1920,512]{1,0:T(8,128)}) fusion(bf16[2,512,512]{2,1,0:T(8,128)(2,1)} %param.27, f32[1920,512]{1,0:T(8,128)} %add.212, f32[1920,512]{1,0:T(8,128)} %gather_fusion, bf16[1920,512]{1,0:T(8,128)(2,1)S(1)} %copy-done.2, pred[1920]{0:T(1024)(128)(4,1)S(1)} %copy-done.26, bf16[2,1536,512]{2,1,0:T(8,128)(2,1)} %param.26), kind=kOutput, calls=%fused_computation.210 | convolution fusion | flops 2022111360 | bytes 14820736 | tf_op jit(solution)/shard_map/dot_general | solution.py:50
  90.7 2.8 %multiply_reduce_fusion.1 = f32[1920]{0:T(1024)S(1)} fusion(f32[1920,512]{1,0:T(8,128)} %get-tuple-element.31, f32[1920]{0:T(1024)S(1)} %broadcast_multiply_fusion.1), kind=kLoop, calls=%fused_computation.21 | loop fusion | flops 2947200 | bytes 3947520 | tf_op jit(solution)/shard_map/reduce_sum | solution.py:44
  93.5 3.6 %reshape.188 = bf16[2560,512]{1,0:T(8,128)(2,1)S(1)} reshape(bf16[128,20,512]{2,1,0:T(8,128)(2,1)} %all-to-all-done.1) | data formatting | bytes 5242880 | tf_op jit(solution)/shard_map/reshape | solution.py:12
  97.2 1.6 gather_fusion.2
  98.8 1.6 gather_fusion.3
  100.4 1.4 convolution_add_fusion.5
  101.8 1.9 fusion.147
  104.1 1.4 scatter_custom_fusion.1
  106.6 19.3 %all-to-all-start.2 = ((bf16[128,3,512]{2,1,0:T(4,128)(2,1)}), bf16[128,3,512]{2,1,0:T(4,128)(2,1)S(1)}, u32[]{:S(2)}, u32[]{:S(2)}) async-start(bf16[128,3,512]{2,1,0:T(4,128)(2,1)} %reshape.189), calls=%async_computation.2 | async-start | bytes 1048576 | tf_op jit(solution)/shard_map/all_to_all | solution.py:80
  125.9 3.4 %add_convert_fusion.1 = bf16[1920,512]{1,0:T(8,128)(2,1)S(1)} fusion(bf16[1920,512]{1,0:T(8,128)(2,1)} %reshape.183, f32[1920,512]{1,0:T(8,128)} %get-tuple-element.31, f32[512]{0:T(512)S(1)} %bitcast.130, f32[1920]{0:T(1024)S(1)} %add_rsqrt_fusion.1, f32[1920]{0:T(1024)S(1)} %broadcast_multiply_fusion.1), kind=kLoop, calls=%fused_computation.20 | loop fusion | flops 5898240 | bytes 7881728 | tf_op jit(solution)/shard_map/convert_element_type | solution.py:51
  129.3 2.9 %reshape.198 = f32[320,6,512]{2,1,0:T(8,128)} reshape(bf16[1920,512]{1,0:T(8,128)(2,1)S(1)} %add_convert_fusion.1) | data formatting | bytes 5898240 | tf_op jit(solution)/shard_map/convert_element_type | solution.py:163
  132.1 5.0 %reduce_sum.141 = f32[320,512]{1,0:T(8,128)} reduce(f32[320,6,512]{2,1,0:T(8,128)} %reshape.198, f32[]{:T(128)} %constant.121.clone.1), dimensions={1}, to_apply=%region_2.4 | reduce | flops 819200 | bytes 4587524 | tf_op jit(solution)/shard_map/reduce_sum | solution.py:163
  137.1 2.0 fusion.20
  140.5 1.3 fusion.89
  141.8 2.6 scatter_fusion
  144.4 2.3 fusion.152
  147.2 2.2 fusion.24
  150.1 1.1 collective-permute-start.4
  151.2 3.8 %collective-permute-start.5 = (bf16[1,20,512]{2,1,0:T(8,128)(2,1)S(1)}, bf16[1,20,512]{2,1,0:T(8,128)(2,1)S(1)}, u32[]{:S(2)}, u32[]{:S(2)}) collective-permute-start(bf16[1,20,512]{2,1,0:T(8,128)(2,1)S(1)} %get-tuple-element.19), channel_id=1, source_target_pairs={{8,0},{16,8},{24,16},{32,24},{40,32},{48,40},{56,48},{64,56},{72,6... | collective-permute-start | bytes 61448 | tf_op jit(solution)/shard_map/ppermute | solution.py:35
  155.1 1.9 stack.5
  156.9 7.1 %all-to-all-start.3 = ((bf16[128,20,512]{2,1,0:T(8,128)(2,1)}), bf16[128,20,512]{2,1,0:T(8,128)(2,1)}, u32[]{:S(2)}, u32[]{:S(2)}) async-start(bf16[128,20,512]{2,1,0:T(8,128)(2,1)} %stack.5), calls=%async_computation.3 | async-start | bytes 6291456 | tf_op jit(solution)/shard_map/all_to_all | solution.py:13
  164.2 1.4 collective-permute-start.7
  166.0 1.4 fusion.15
  167.3 3.0 %add.231 = f32[320,6,512]{2,1,0:T(8,128)} broadcast(f32[320,512]{1,0:T(8,128)S(1)} %fusion.15), dimensions={0,2} | broadcast | bytes 4587520 | tf_op jit(solution)/shard_map/add | solution.py:149
  170.3 5.5 %add.232 = f32[1920,512]{1,0:T(8,128)} reshape(f32[320,6,512]{2,1,0:T(8,128)} %add.231) | data formatting | bytes 7864320 | tf_op jit(solution)/shard_map/add | solution.py:149
  176.3 1.4 fusion.18
  177.7 6.4 %gather_fusion.4 = f32[1920,512]{1,0:T(8,128)} fusion(f32[396,512]{1,0:T(8,128)S(1)} %fusion.18, s32[2048]{0:T(1024)} %copy-done.10), kind=kCustom, calls=%fused_computation.3.clone | custom fusion | bytes 7872000 | tf_op jit(solution)/shard_map/jit(_take)/gather | solution.py:145
  184.1 8.1 %fusion.157 = (f32[1920]{0:T(1024)S(1)}, f32[1920,512]{1,0:T(8,128)}) fusion(bf16[2,512,512]{2,1,0:T(8,128)(2,1)} %param.27, f32[1920,512]{1,0:T(8,128)} %add.232, f32[1920,512]{1,0:T(8,128)} %gather_fusion.4, pred[1920]{0:T(1024)(128)(4,1)S(1)} %copy-done.27, bf16[1920,512]{1,0:T(8,128)(2,1)S(1)} %add_convert_fusion.1, bf16[2,1536,512]{2,1,0:T(8,128)(2,1)} %param.26), kind=kOutput, calls=%fused_computation.213 | convolution fusion | flops 2022111360 | bytes 14820736 | tf_op jit(solution)/shard_map/dot_general | solution.py:50
  192.2 2.8 %multiply_reduce_fusion = f32[1920]{0:T(1024)S(1)} fusion(f32[1920,512]{1,0:T(8,128)} %get-tuple-element.37, f32[1920]{0:T(1024)S(1)} %broadcast_multiply_fusion), kind=kLoop, calls=%fused_computation.18 | loop fusion | flops 2947200 | bytes 3947520 | tf_op jit(solution)/shard_map/reduce_sum | solution.py:44
  195.1 10.1 %all-to-all-done.3 = bf16[128,20,512]{2,1,0:T(8,128)(2,1)} async-done(((bf16[128,20,512]{2,1,0:T(8,128)(2,1)}), bf16[128,20,512]{2,1,0:T(8,128)(2,1)}, u32[]{:S(2)}, u32[]{:S(2)}) %all-to-all-start.3) | async-done | bytes 2621472 | tf_op jit(solution)/shard_map/all_to_all | solution.py:13
  205.1 5.2 %reshape.193 = bf16[2560,512]{1,0:T(8,128)(2,1)} reshape(bf16[128,20,512]{2,1,0:T(8,128)(2,1)} %all-to-all-done.3) | data formatting | bytes 5242880 | tf_op jit(solution)/shard_map/reshape | solution.py:12
  210.3 3.2 %gather_fusion.6 = bf16[160,512]{1,0:T(8,128)(2,1)S(1)} fusion(bf16[2560,512]{1,0:T(8,128)(2,1)} %reshape.193, s32[1024]{0:T(1024)} %copy-done.15), kind=kCustom, calls=%fused_computation.6.clone | custom fusion | bytes 328320 | tf_op jit(solution)/shard_map/jit(_take)/gather | solution.py:154
  213.5 3.2 %gather_fusion.7 = bf16[160,512]{1,0:T(8,128)(2,1)S(1)} fusion(bf16[2560,512]{1,0:T(8,128)(2,1)} %reshape.193, s32[1024]{0:T(1024)} %copy-done.14), kind=kCustom, calls=%fused_computation.7.clone | custom fusion | bytes 328320 | tf_op jit(solution)/shard_map/jit(_take)/gather | solution.py:157
  216.7 1.3 convolution_add_fusion.3
  218.1 1.8 fusion.160
  220.3 1.4 scatter_custom_fusion.3
  222.8 22.9 %all-to-all-start.4 = ((bf16[128,3,512]{2,1,0:T(4,128)(2,1)}), bf16[128,3,512]{2,1,0:T(4,128)(2,1)}, u32[]{:S(2)}, u32[]{:S(2)}) async-start(bf16[128,3,512]{2,1,0:T(4,128)(2,1)} %reshape.194), calls=%async_computation.4 | async-start | bytes 1048576 | tf_op jit(solution)/shard_map/all_to_all | solution.py:80
  245.7 3.7 %add_convert_fusion = bf16[1920,512]{1,0:T(8,128)(2,1)} fusion(f32[1920,512]{1,0:T(8,128)} %get-tuple-element.37, f32[512]{0:T(512)S(1)} %bitcast.128, f32[1920]{0:T(1024)S(1)} %add_rsqrt_fusion, f32[1920]{0:T(1024)S(1)} %broadcast_multiply_fusion, bf16[1920,512]{1,0:T(8,128)(2,1)S(1)} %add_convert_fusion.1), kind=kLoop, calls=%fused_computation.17 | loop fusion | flops 5898240 | bytes 7881728 | tf_op jit(solution)/shard_map/convert_element_type | solution.py:51
  249.4 4.6 %reshape.201 = f32[320,6,512]{2,1,0:T(8,128)} reshape(bf16[1920,512]{1,0:T(8,128)(2,1)} %add_convert_fusion) | data formatting | bytes 5898240 | tf_op jit(solution)/shard_map/convert_element_type | solution.py:163
  254.1 2.3 reshape.197
  256.3 5.1 %reduce_sum.149 = f32[320,512]{1,0:T(8,128)} reduce(f32[320,6,512]{2,1,0:T(8,128)} %reshape.201, f32[]{:T(128)} %constant.121.clone.1), dimensions={1}, to_apply=%region_15.19 | reduce | flops 819200 | bytes 4587524 | tf_op jit(solution)/shard_map/reduce_sum | solution.py:163
  261.5 2.4 copy.36
  263.9 1.4 reshape.195
  265.6 2.6 scatter_fusion.1
  268.2 2.3 fusion.165
  (150 shorter events, 18.4 us)
Async XLA Ops:
  2.3 61.4 %collective-permute-start.1 = (bf16[1,20,512]{2,0,1:T(2,128)(2,1)}, bf16[1,20,512]{2,0,1:T(2,128)(2,1)S(1)}, u32[]{:S(2)}, u32[]{:S(2)}) collective-permute-start(bf16[1,20,512]{2,0,1:T(2,128)(2,1)} %get-tuple-element.22), channel_id=1, source_target_pairs={{8,0},{16,8},{24,16},{32,24},{40,32},{48,40},{56,48},{64,56},{72,6... | collective-permute-start | bytes 61448 | tf_op jit(solution)/shard_map/ppermute | solution.py:35
  8.1 55.6 %collective-permute-start = (bf16[1,20,512]{2,0,1:T(2,128)(2,1)S(1)}, bf16[1,20,512]{2,0,1:T(2,128)(2,1)S(1)}, u32[]{:S(2)}, u32[]{:S(2)}) collective-permute-start(bf16[1,20,512]{2,0,1:T(2,128)(2,1)S(1)} %get-tuple-element.21), channel_id=1, source_target_pairs={{0,8},{8,16},{16,24},{24,32},{32,40},{40,48},{48,56},{56,64},{64,7... | collective-permute-start | bytes 61448 | tf_op jit(solution)/shard_map/ppermute | solution.py:33
  8.9 25.1 %copy-start.20 = (f32[2,512]{1,0:T(2,128)S(1)}, f32[2,512]{1,0:T(2,128)}, u32[]{:S(2)}) copy-start(f32[2,512]{1,0:T(2,128)} %param.28) | copy-start | bytes 12292
  8.9 25.7 %copy-start.7 = (bf16[160,512]{1,0:T(8,128)(2,1)S(1)}, bf16[160,512]{1,0:T(8,128)(2,1)}, u32[]{:S(2)}) copy-start(bf16[160,512]{1,0:T(8,128)(2,1)} %param.21) | copy-start | bytes 491524
  9.3 15.1 %copy-start.28 = (s32[160]{0:T(256)}, s32[160]{0:T(256)S(1)}, u32[]{:S(2)}) copy-start(s32[160]{0:T(256)S(1)} %compare_select_fusion.3) | copy-start | bytes 1924
  11.3 25.8 %all-to-all-start = ((bf16[128,1,3]{2,1,0:T(2,128)(2,1)}), bf16[128,1,3]{2,1,0:T(2,128)(2,1)S(1)}, u32[]{:S(2)}, u32[]{:S(2)}) async-start(bf16[128,1,3]{2,1,0:T(2,128)(2,1)} %all_to_all.25), calls=%async_computation | async-start | bytes 131072 | tf_op jit(solution)/shard_map/all_to_all | solution.py:87
  22.0 14.5 %copy-start.21 = (f32[2,512]{1,0:T(2,128)S(1)}, f32[2,512]{1,0:T(2,128)}, u32[]{:S(2)}) copy-start(f32[2,512]{1,0:T(2,128)} %param.31) | copy-start | bytes 12292
  25.7 11.4 %copy-start.17 = (s32[20]{0:T(128)}, s32[20]{0:T(128)S(1)}, u32[]{:S(2)}) copy-start(s32[20]{0:T(128)S(1)} %compare_select_fusion.4) | copy-start | bytes 244
  26.3 12.7 %copy-start.24 = (pred[20]{0:T(512)(128)(4,1)}, pred[20]{0:T(512)(128)(4,1)S(1)}, u32[]{:S(2)}) copy-start(pred[20]{0:T(512)(128)(4,1)S(1)} %compare_and_fusion.3) | copy-start | bytes 64
  37.2 39.2 %copy-start.10 = (s32[2048]{0:T(1024)}, s32[2048]{0:T(1024)S(1)}, u32[]{:S(2)}) copy-start(s32[2048]{0:T(1024)S(1)} %pad_clamp_fusion) | copy-start | bytes 24580
  39.0 54.5 %all-to-all-start.1 = ((bf16[128,20,512]{2,1,0:T(8,128)(2,1)}), bf16[128,20,512]{2,1,0:T(8,128)(2,1)}, u32[]{:S(2)}, u32[]{:S(2)}) async-start(bf16[128,20,512]{2,1,0:T(8,128)(2,1)} %stack.4), calls=%async_computation.1 | async-start | bytes 6291456 | tf_op jit(solution)/shard_map/all_to_all | solution.py:13
  49.2 48.0 %copy-start.15 = (s32[1024]{0:T(1024)}, s32[1024]{0:T(1024)S(1)}, u32[]{:S(2)}) copy-start(s32[1024]{0:T(1024)S(1)} %get-tuple-element.43) | copy-start | bytes 12292
  49.2 49.5 %copy-start.14 = (s32[1024]{0:T(1024)}, s32[1024]{0:T(1024)S(1)}, u32[]{:S(2)}) copy-start(s32[1024]{0:T(1024)S(1)} %get-tuple-element.42) | copy-start | bytes 12292
  58.1 5.6 %copy-start.3 = (bf16[16,20,512]{2,0,1:T(8,128)(2,1)S(1)}, bf16[16,20,512]{2,0,1:T(8,128)(2,1)}, u32[]{:S(2)}) copy-start(bf16[16,20,512]{2,0,1:T(8,128)(2,1)} %param.19) | copy-start | bytes 983044
  63.7 10.7 %collective-permute-start.3 = (bf16[18,1,512]{2,0,1:T(8,128)(2,1)S(1)}, bf16[18,1,512]{2,0,1:T(8,128)(2,1)S(1)}, u32[]{:S(2)}, u32[]{:S(2)}) collective-permute-start(bf16[18,1,512]{2,0,1:T(8,128)(2,1)S(1)} %get-tuple-element.18), channel_id=1, source_target_pairs={{1,0},{2,1},{3,2},{4,3},{5,4},{6,5},{7,6},{0,7},{9,8},{10,9},{11,1... | collective-permute-start | bytes 55304 | tf_op jit(solution)/shard_map/ppermute | solution.py:35
  65.1 9.4 %collective-permute-start.2 = (bf16[18,1,512]{2,0,1:T(8,128)(2,1)S(1)}, bf16[18,1,512]{2,0,1:T(8,128)(2,1)S(1)}, u32[]{:S(2)}, u32[]{:S(2)}) collective-permute-start(bf16[18,1,512]{2,0,1:T(8,128)(2,1)S(1)} %get-tuple-element.17), channel_id=1, source_target_pairs={{0,1},{1,2},{2,3},{3,4},{4,5},{5,6},{6,7},{7,0},{8,9},{9,10},{10,1... | collective-permute-start | bytes 55304 | tf_op jit(solution)/shard_map/ppermute | solution.py:33
  66.0 74.6 %copy-start.11 = (s32[384]{0:T(512)}, s32[384]{0:T(512)S(1)}, u32[]{:S(2)}) copy-start(s32[384]{0:T(512)S(1)} %reshape.200) | copy-start | bytes 4612
  76.4 6.2 %copy-start.2 = (bf16[1920,512]{1,0:T(8,128)(2,1)S(1)}, bf16[1920,512]{1,0:T(8,128)(2,1)}, u32[]{:S(2)}) copy-start(bf16[1920,512]{1,0:T(8,128)(2,1)} %reshape.183) | copy-start | bytes 5898244
  76.4 6.2 %copy-start.26 = (pred[1920]{0:T(1024)(128)(4,1)S(1)}, pred[1920]{0:T(1024)(128)(4,1)}, u32[]{:S(2)}) copy-start(pred[1920]{0:T(1024)(128)(4,1)} %compare_and_fusion) | copy-start | bytes 5764
  93.5 6.9 %copy-start.22 = (pred[160]{0:T(512)(128)(4,1)S(1)}, pred[160]{0:T(512)(128)(4,1)}, u32[]{:S(2)}) copy-start(pred[160]{0:T(512)(128)(4,1)} %compare_and_fusion.2) | copy-start | bytes 484
  97.2 4.7 %copy-start.29 = (pred[160]{0:T(512)(128)(4,1)S(1)}, pred[160]{0:T(512)(128)(4,1)}, u32[]{:S(2)}) copy-start(pred[160]{0:T(512)(128)(4,1)} %compare_and_fusion.1) | copy-start | bytes 484
  98.8 5.2 %copy-start.8 = (bf16[160,512]{1,0:T(8,128)(2,1)S(1)}, bf16[160,512]{1,0:T(8,128)(2,1)}, u32[]{:S(2)}) copy-start(bf16[160,512]{1,0:T(8,128)(2,1)} %param.21) | copy-start | bytes 491524
  104.1 33.0 %copy-start.4 = (bf16[160,512]{1,0:T(8,128)(2,1)}, bf16[160,512]{1,0:T(8,128)(2,1)S(1)}, u32[]{:S(2)}) copy-start(bf16[160,512]{1,0:T(8,128)(2,1)S(1)} %add_convert_fusion.5) | copy-start | bytes 491524
  106.6 32.9 %all-to-all-start.2 = ((bf16[128,3,512]{2,1,0:T(4,128)(2,1)}), bf16[128,3,512]{2,1,0:T(4,128)(2,1)S(1)}, u32[]{:S(2)}, u32[]{:S(2)}) async-start(bf16[128,3,512]{2,1,0:T(4,128)(2,1)} %reshape.189), calls=%async_computation.2 | async-start | bytes 1048576 | tf_op jit(solution)/shard_map/all_to_all | solution.py:80
  132.1 9.7 %copy-start.18 = (s32[20]{0:T(128)S(1)}, s32[20]{0:T(128)}, u32[]{:S(2)}) copy-start(s32[20]{0:T(128)} %copy-done.17) | copy-start | bytes 244
  146.7 8.3 %copy-start.25 = (pred[20]{0:T(512)(128)(4,1)S(1)}, pred[20]{0:T(512)(128)(4,1)}, u32[]{:S(2)}) copy-start(pred[20]{0:T(512)(128)(4,1)} %copy-done.24) | copy-start | bytes 64
  150.1 13.9 %collective-permute-start.4 = (bf16[1,20,512]{2,1,0:T(8,128)(2,1)S(1)}, bf16[1,20,512]{2,1,0:T(8,128)(2,1)S(1)}, u32[]{:S(2)}, u32[]{:S(2)}) collective-permute-start(bf16[1,20,512]{2,1,0:T(8,128)(2,1)S(1)} %get-tuple-element.20), channel_id=1, source_target_pairs={{0,8},{8,16},{16,24},{24,32},{32,40},{40,48},{48,56},{56,64},{64,7... | collective-permute-start | bytes 61448 | tf_op jit(solution)/shard_map/ppermute | solution.py:33
  151.2 12.8 %collective-permute-start.5 = (bf16[1,20,512]{2,1,0:T(8,128)(2,1)S(1)}, bf16[1,20,512]{2,1,0:T(8,128)(2,1)S(1)}, u32[]{:S(2)}, u32[]{:S(2)}) collective-permute-start(bf16[1,20,512]{2,1,0:T(8,128)(2,1)S(1)} %get-tuple-element.19), channel_id=1, source_target_pairs={{8,0},{16,8},{24,16},{32,24},{40,32},{48,40},{56,48},{64,56},{72,6... | collective-permute-start | bytes 61448 | tf_op jit(solution)/shard_map/ppermute | solution.py:35
  156.9 48.2 %all-to-all-start.3 = ((bf16[128,20,512]{2,1,0:T(8,128)(2,1)}), bf16[128,20,512]{2,1,0:T(8,128)(2,1)}, u32[]{:S(2)}, u32[]{:S(2)}) async-start(bf16[128,20,512]{2,1,0:T(8,128)(2,1)} %stack.5), calls=%async_computation.3 | async-start | bytes 6291456 | tf_op jit(solution)/shard_map/all_to_all | solution.py:13
  164.2 11.7 %collective-permute-start.7 = (bf16[18,1,512]{2,1,0:T(2,128)(2,1)S(1)}, bf16[18,1,512]{2,1,0:T(2,128)(2,1)S(1)}, u32[]{:S(2)}, u32[]{:S(2)}) collective-permute-start(bf16[18,1,512]{2,1,0:T(2,128)(2,1)S(1)} %get-tuple-element.16), channel_id=1, source_target_pairs={{1,0},{2,1},{3,2},{4,3},{5,4},{6,5},{7,6},{0,7},{9,8},{10,9},{11,1... | collective-permute-start | bytes 55304 | tf_op jit(solution)/shard_map/ppermute | solution.py:35
  165.6 10.3 %collective-permute-start.6 = (bf16[18,1,512]{2,1,0:T(2,128)(2,1)S(1)}, bf16[18,1,512]{2,1,0:T(2,128)(2,1)S(1)}, u32[]{:S(2)}, u32[]{:S(2)}) collective-permute-start(bf16[18,1,512]{2,1,0:T(2,128)(2,1)S(1)} %get-tuple-element.15), channel_id=1, source_target_pairs={{0,1},{1,2},{2,3},{3,4},{4,5},{5,6},{6,7},{7,0},{8,9},{9,10},{10,1... | collective-permute-start | bytes 55304 | tf_op jit(solution)/shard_map/ppermute | solution.py:33
  177.7 6.4 %copy-start.27 = (pred[1920]{0:T(1024)(128)(4,1)S(1)}, pred[1920]{0:T(1024)(128)(4,1)}, u32[]{:S(2)}) copy-start(pred[1920]{0:T(1024)(128)(4,1)} %compare_and_fusion) | copy-start | bytes 5764
  195.0 21.7 %copy-start.6 = (f32[160,512]{1,0:T(8,128)S(1)}, f32[160,512]{1,0:T(8,128)}, u32[]{:S(2)}) copy-start(f32[160,512]{1,0:T(8,128)} %fusion.20) | copy-start | bytes 983044
  195.1 21.7 %copy-start.23 = (pred[160]{0:T(512)(128)(4,1)S(1)}, pred[160]{0:T(512)(128)(4,1)}, u32[]{:S(2)}) copy-start(pred[160]{0:T(512)(128)(4,1)} %compare_and_fusion.2) | copy-start | bytes 484
  210.3 7.8 %copy-start.30 = (pred[160]{0:T(512)(128)(4,1)S(1)}, pred[160]{0:T(512)(128)(4,1)}, u32[]{:S(2)}) copy-start(pred[160]{0:T(512)(128)(4,1)} %compare_and_fusion.1) | copy-start | bytes 484
  213.5 6.7 %copy-start.5 = (bf16[160,512]{1,0:T(8,128)(2,1)S(1)}, bf16[160,512]{1,0:T(8,128)(2,1)}, u32[]{:S(2)}) copy-start(bf16[160,512]{1,0:T(8,128)(2,1)} %copy-done.4) | copy-start | bytes 491524
  213.5 6.7 %copy-start.13 = (f32[1,512]{1,0:T(1,128)S(1)}, f32[1,512]{1,0:T(1,128)}, u32[]{:S(2)}) copy-start(f32[1,512]{1,0:T(1,128)} %get-tuple-element.25) | copy-start | bytes 6148
  220.3 29.1 %copy-start.9 = (bf16[160,512]{1,0:T(8,128)(2,1)}, bf16[160,512]{1,0:T(8,128)(2,1)S(1)}, u32[]{:S(2)}) copy-start(bf16[160,512]{1,0:T(8,128)(2,1)S(1)} %add_convert_fusion.4) | copy-start | bytes 491524
  222.8 41.0 %all-to-all-start.4 = ((bf16[128,3,512]{2,1,0:T(4,128)(2,1)}), bf16[128,3,512]{2,1,0:T(4,128)(2,1)}, u32[]{:S(2)}, u32[]{:S(2)}) async-start(bf16[128,3,512]{2,1,0:T(4,128)(2,1)} %reshape.194), calls=%async_computation.4 | async-start | bytes 1048576 | tf_op jit(solution)/shard_map/all_to_all | solution.py:80
  249.4 4.7 %copy-start = (bf16[1920,512]{1,0:T(8,128)(2,1)S(1)}, bf16[1920,512]{1,0:T(8,128)(2,1)}, u32[]{:S(2)}) copy-start(bf16[1920,512]{1,0:T(8,128)(2,1)} %add_convert_fusion) | copy-start | bytes 5898244
  256.3 5.2 %copy-start.1 = (bf16[16,20,6,512]{3,2,1,0:T(8,128)(2,1)S(1)}, bf16[16,20,6,512]{3,2,1,0:T(8,128)(2,1)}, u32[]{:S(2)}) copy-start(bf16[16,20,6,512]{3,2,1,0:T(8,128)(2,1)} %reshape.197) | copy-start | bytes 5898244
  261.5 3.8 %copy-start.12 = (s32[384]{0:T(512)S(1)}, s32[384]{0:T(512)}, u32[]{:S(2)}) copy-start(s32[384]{0:T(512)} %copy-done.11) | copy-start | bytes 4612
  261.5 4.1 %copy-start.19 = (s32[20]{0:T(128)S(1)}, s32[20]{0:T(128)}, u32[]{:S(2)}) copy-start(s32[20]{0:T(128)} %copy-done.17) | copy-start | bytes 244
  265.5 5.2 %copy-start.16 = (f32[1,512]{1,0:T(1,128)S(1)}, f32[1,512]{1,0:T(1,128)}, u32[]{:S(2)}) copy-start(f32[1,512]{1,0:T(1,128)} %get-tuple-element.23) | copy-start | bytes 6148
